TPU v7x, 32 devices: a whole 2x2x4 slice. The times are simulated.
32 devices in a mesh: groups: 2 (over x), seq: 8 (over z, y), sub: 2 (over core).
Axes of the slice: x: 2, y: 2, z: 4, core: 2. Of those that a mesh axis runs over, the one named last changes fastest.
Arguments:
- frames: bfloat16 [2048, 1024], P(('groups', 'seq', 'sub')), parts along dimension 0, may hold values from -6 to 6
- fine_gain: float32 [1024], replicated, may hold values from 0.1 to 1.9
- dw_kernel: bfloat16 [5, 1024], replicated, may hold values from -3 to 3
- w_down: bfloat16 [4096, 4096], P(None, 'seq'), may hold values from -0.21875 to 0.21875
- coarse_gain: float32 [4096], replicated, may hold values from 0.1 to 1.9
- w_qkv: bfloat16 [3, 4096, 4096], P(None, None, 'seq'), may hold values from -1.609375 to 1.609375
- w_out: bfloat16 [4096, 4096], P('seq'), may hold values from -0.09375 to 0.09375
- w_up: bfloat16 [4096, 4096], P('seq'), may hold values from -0.09375 to 0.09375
Outputs:
- denoised: bfloat16 [2048, 1024], P(('groups', 'seq', 'sub')), parts along dimension 0
There are 2 independent parts, one for each index of `groups`. A program takes and returns all parts, laid end to end along the dimension named above; an argument that names none is the same for every part. Nothing has to cross between parts.
All inputs are finite; a program needn't handle non-finite values.
Results may differ from a plain program's by a relative error of at most 0.012.
Values may be sent and summed in bfloat16 or wider, within the bound.
No kernel may reach another device: no remote copies, remote signals or barrier semaphores. Data moves between devices by JAX's collectives and lax.ppermute only.
A program may use at most 128 MiB of HBM per device.

v0:
```python
import math
import jax
import jax.numpy as jnp
from jax import lax
from jax.sharding import PartitionSpec as P

DF = 1024
HD = 128
KW = 5
epsilon = 1e-06


def padded_2(array, sides, width):
    for axis, dim in sides:
        size, length = (lax.axis_size(axis), array.shape[dim])
        up = [(i, (i + 1) % size) for i in range(size - 1)]
        down = [(j, i) for i, j in up]
        last = lax.slice_in_dim(array, length - width, length, axis=dim)
        leading = lax.slice_in_dim(array, 0, width, axis=dim)
        before = lax.ppermute(last, axis, up)
        after = lax.ppermute(leading, axis, down)
        array = jnp.concatenate([before, array, after], axis=dim)
    return array


def partner(value, axis, bit):
    mask = 2**bit
    pairs = [(source, source ^ mask) for source in range(lax.axis_size(axis))]
    return lax.ppermute(value, axis, pairs)


def attend(queries, keys_all, values_all, heads_here):
    row_total = queries.shape[0]
    block_rows = min(row_total, 512)
    key_heads = keys_all.reshape(keys_all.shape[0], heads_here, HD)
    value_heads = values_all.reshape(values_all.shape[0], heads_here, HD)
    query_blocks = queries.reshape(row_total // block_rows, block_rows, heads_here, HD)
    score_scale = 1.0 / math.sqrt(HD)

    def one_block(query_block):
        scores = (
            jnp.einsum("qhd,khd->hqk", query_block, key_heads, preferred_element_type=jnp.float32)
            * score_scale
        )
        peak = jnp.max(scores, axis=2, keepdims=True)
        weights = jnp.exp(scores - peak)
        weights = (weights / jnp.sum(weights, axis=2, keepdims=True)).astype(jnp.bfloat16)
        return jnp.einsum(
            "hqk,khd->qhd", weights, value_heads, preferred_element_type=jnp.float32
        ).astype(jnp.bfloat16)

    outputs = lax.map(one_block, query_blocks)
    return outputs.reshape(row_total, heads_here * HD)


def per_device(frames, fine_gain, dw_kernel, w_down, coarse_gain, w_qkv, w_out, w_up):
    frame_rows = frames.shape[0]
    heads_here = w_qkv.shape[2] // HD
    frames_f32 = frames.astype(jnp.float32)
    normed_fine = (
        frames_f32
        * lax.rsqrt(jnp.mean(frames_f32 * frames_f32, axis=1, keepdims=True) + epsilon)
        * fine_gain
    ).astype(jnp.bfloat16)
    padded = padded_2(normed_fine, ((("seq", "sub"), 0),), KW // 2)
    convolved = jnp.zeros((frame_rows, DF), jnp.float32)
    for offset in range(KW):
        convolved = convolved + padded[offset : offset + frame_rows].astype(
            jnp.float32
        ) * dw_kernel[offset].astype(jnp.float32)
    patches = convolved.astype(jnp.bfloat16).reshape(frame_rows // 4, 4 * DF)
    coarse = jnp.dot(
        lax.all_gather(patches, "seq", axis=0, tiled=True),
        w_down,
        preferred_element_type=jnp.float32,
    ).astype(jnp.bfloat16)
    coarse_f32 = coarse.astype(jnp.float32)
    whole = lax.all_gather(coarse, "seq", axis=1, tiled=True).astype(jnp.float32)
    normed_coarse = (
        whole * lax.rsqrt(jnp.mean(whole * whole, axis=1, keepdims=True) + epsilon) * coarse_gain
    ).astype(jnp.bfloat16)
    queries = jnp.dot(normed_coarse, w_qkv[0], preferred_element_type=jnp.float32).astype(
        jnp.bfloat16
    )
    own_keys = jnp.dot(normed_coarse, w_qkv[1], preferred_element_type=jnp.float32).astype(
        jnp.bfloat16
    )
    own_values = jnp.dot(normed_coarse, w_qkv[2], preferred_element_type=jnp.float32).astype(
        jnp.bfloat16
    )
    other_keys, other_values = partner((own_keys, own_values), "sub", 0)
    keys_all = jnp.concatenate([own_keys, other_keys], axis=0)
    values_all = jnp.concatenate([own_values, other_values], axis=0)
    attended = attend(queries, keys_all, values_all, heads_here)
    partial_out = jnp.dot(attended, w_out, preferred_element_type=jnp.float32)
    projected = lax.psum_scatter(
        partial_out.astype(jnp.bfloat16), "seq", scatter_dimension=1, tiled=True
    ).astype(jnp.float32)
    mixed = (coarse_f32 + projected).astype(jnp.bfloat16)
    lifted = lax.psum_scatter(
        jnp.dot(mixed, w_up, preferred_element_type=jnp.float32),
        "seq",
        scatter_dimension=0,
        tiled=True,
    )
    return (frames_f32 + lifted.reshape(frame_rows, DF)).astype(jnp.bfloat16)


def solution(mesh):
    placed = (
        P(("groups", "seq", "sub"), None),
        P(),
        P(),
        P(None, "seq"),
        P(),
        P(None, None, "seq"),
        P("seq", None),
        P("seq", None),
    )
    return jax.shard_map(
        per_device,
        mesh=mesh,
        in_specs=placed,
        out_specs=P(("groups", "seq", "sub"), None),
        check_vma=False,
    )
```

profile of v0, /device:TPU:0, one launch (start us, length us, event | category | flops | bytes accessed | tf_op | source)
XLA Modules:
  0.0 262.8 jit_solution(18423422648642373346)
XLA Ops:
  6.5 0.0 copy-start.3
  6.5 0.0 all-gather.3.cloned.1.call-start
  6.5 1.0 fusion.27
  7.6 1.0 fusion.29
  8.6 2.4 collective-permute-start
  11.0 1.3 collective-permute-start.1
  12.3 0.9 slice_convert_fusion.4
  13.2 0.0 collective-permute-done
  13.2 3.0 %collective-permute-done.1 = bf16[2,1024]{1,0:T(2,128)(2,1)S(1)} collective-permute-done((bf16[2,1024]{1,0:T(2,128)(2,1)S(1)}, bf16[2,1024]{1,0:T(2,128)(2,1)S(1)}, u32[]{:S(2)}, u32[]{:S(2)}) %collective-permute-start.1) | collective-permute-done | bytes 4128 | tf_op jit(solution)/shard_map/ppermute | solution.py:21
  16.2 0.2 add_convert_fusion.1
  16.4 0.7 reshape.38
  17.1 0.0 all-gather.3.cloned.1.call-update
  17.1 0.0 all-gather.5.cloned.1.call-start
  17.2 43.4 %all-gather.3.cloned.1.call-done = bf16[128,4096]{1,0:T(8,128)(2,1)} async-done(((bf16[16,4096]{1,0:T(8,128)(2,1)}), bf16[128,4096]{1,0:T(8,128)(2,1)}) %all-gather.3.cloned.1.call-update) | async-done | bytes 1048592 | tf_op jit(solution)/shard_map/all_gather | solution.py:73
  60.6 3.9 %convolution_convert_fusion.2 = bf16[128,512]{1,0:T(8,128)(2,1)} fusion(bf16[128,4096]{1,0:T(8,128)(2,1)} %all-gather.3.cloned.1.call-done, bf16[4096,512]{1,0:T(8,128)(2,1)} %param.11), kind=kOutput, calls=%fused_computation.23 | convolution fusion | flops 536936448 | bytes 5373952 | tf_op jit(solution)/shard_map/dot_general | solution.py:72
  64.5 0.0 all-gather.5.cloned.1.call-update
  64.5 0.0 reduce-scatter.3.cloned.1.call-start
  64.6 38.4 %all-gather.5.cloned.1.call-done = bf16[128,4096]{1,0:T(8,128)(2,1)} async-done(((bf16[128,512]{1,0:T(8,128)(2,1)}), bf16[128,4096]{1,0:T(8,128)(2,1)}) %all-gather.5.cloned.1.call-update) | async-done | bytes 1048592 | tf_op jit(solution)/shard_map/all_gather | solution.py:78
  103.0 0.0 copy-start.2
  103.0 1.6 fusion.10
  104.6 0.0 copy-done.3
  104.6 3.3 %fusion.15 = bf16[128,512]{1,0:T(8,128)(2,1)S(1)} fusion(bf16[3,4096,512]{2,1,0:T(8,128)(2,1)} %param.13, bf16[128,4096]{1,0:T(8,128)(2,1)} %all-gather.5.cloned.1.call-done, f32[4096]{0:T(1024)S(1)} %copy-done.3, f32[128]{0:T(128)S(1)} %add_rsqrt_fusion), kind=kOutput, calls=%fused_computation.19 | convolution fusion | flops 539033600 | bytes 5390848 | tf_op jit(solution)/shard_map/dot_general | solution.py:88
  107.9 0.1 collective-permute-start.2
  107.9 0.0 copy-done.2
  107.9 3.0 %fusion.21 = bf16[128,512]{1,0:T(8,128)(2,1)S(1)} fusion(bf16[3,4096,512]{2,1,0:T(8,128)(2,1)} %param.13, bf16[128,4096]{1,0:T(8,128)(2,1)S(1)} %copy-done.2, f32[4096]{0:T(1024)S(1)} %copy-done.3, f32[128]{0:T(128)S(1)} %add_rsqrt_fusion), kind=kOutput, calls=%fused_computation.21 | convolution fusion | flops 539033600 | bytes 5390848 | tf_op jit(solution)/shard_map/dot_general | solution.py:85
  110.9 0.6 collective-permute-start.3
  111.5 2.9 %fusion.24 = bf16[16,4,8,128]{3,2,1,0:T(8,128)(2,1)S(1)} fusion(bf16[3,4096,512]{2,1,0:T(8,128)(2,1)} %param.13, bf16[128,4096]{1,0:T(8,128)(2,1)S(1)} %copy-done.2, f32[4096]{0:T(1024)S(1)} %copy-done.3, f32[128]{0:T(128)S(1)} %add_rsqrt_fusion), kind=kOutput, calls=%fused_computation.24 | convolution fusion | flops 539033600 | bytes 5390848 | tf_op jit(solution)/shard_map/dot_general | solution.py:82
  114.4 0.0 collective-permute-done.2
  114.5 0.1 copy.12
  114.6 0.0 collective-permute-done.3
  114.6 0.4 fusion.49
  115.0 0.2 convolution_multiply_fusion
  115.3 0.0 copy-start.1
  115.3 1.0 convolution_convert_fusion.1
  116.3 3.9 %convolution_convert_fusion = bf16[128,4096]{1,0:T(8,128)(2,1)} fusion(bf16[128,512]{0,1:T(8,128)(2,1)S(1)} %bitcast.57, bf16[512,4096]{1,0:T(8,128)(2,1)} %param.14), kind=kOutput, calls=%fused_computation.1 | convolution fusion | flops 537395200 | bytes 5373952 | tf_op jit(solution)/shard_map/dot_general | solution.py:95
  120.2 0.0 reduce-scatter.3.cloned.1.call-update
  120.3 0.0 copy-start
  120.3 0.0 reduce-scatter.5.cloned.1.call-start
  120.3 62.8 %reduce-scatter.3.cloned.1.call-done = bf16[128,512]{1,0:T(8,128)(2,1)} async-done(((bf16[128,4096]{1,0:T(8,128)(2,1)}), bf16[128,512]{1,0:T(8,128)(2,1)}) %reduce-scatter.3.cloned.1.call-update) | async-done | bytes 131088 | tf_op jit(solution)/shard_map/reduce_scatter | solution.py:96
  183.2 0.0 copy-done.1
  183.2 4.3 %fusion.36 = f32[128,4096]{1,0:T(8,128)} fusion(bf16[512,4096]{1,0:T(8,128)(2,1)} %param.15, bf16[128,512]{1,0:T(8,128)(2,1)} %reduce-scatter.3.cloned.1.call-done, bf16[128,512]{1,0:T(8,128)(2,1)S(1)} %copy-done.1), kind=kOutput, calls=%fused_computation.46 | convolution fusion | flops 537133056 | bytes 6553600 | tf_op jit(solution)/shard_map/dot_general | solution.py:101
  187.5 0.0 reduce-scatter.5.cloned.1.call-update
  187.5 67.0 %reduce-scatter.5.cloned.1.call-done = f32[16,4096]{1,0:T(8,128)} async-done(((f32[128,4096]{1,0:T(8,128)}), f32[16,4096]{1,0:T(8,128)}) %reduce-scatter.5.cloned.1.call-update) | async-done | bytes 262160 | tf_op jit(solution)/shard_map/reduce_scatter | solution.py:100
  254.5 1.0 reshape.42
  255.5 0.0 copy-done
  255.5 0.7 fusion.30
  (4 shorter events, 0.0 us)
Async XLA Ops:
  6.5 98.0 %copy-start.3 = (f32[4096]{0:T(1024)S(1)}, f32[4096]{0:T(1024)}, u32[]{:S(2)}) copy-start(f32[4096]{0:T(1024)} %param.12) | copy-start | bytes 49156
  6.5 54.1 %all-gather.3.cloned.1.call-start = ((), (), s32[]{:S(2)}) async-start(), calls=%async_computation.2 | async-start | bytes 1179648 | tf_op jit(solution)/shard_map/all_gather | solution.py:73
  8.6 4.6 %collective-permute-start = (bf16[2,1024]{1,0:T(2,128)(2,1)S(1)}, bf16[2,1024]{1,0:T(2,128)(2,1)S(1)}, u32[]{:S(2)}, u32[]{:S(2)}) collective-permute-start(bf16[2,1024]{1,0:T(2,128)(2,1)S(1)} %get-tuple-element.13), channel_id=1, source_target_pairs={{0,1},{1,2},{2,3},{3,4},{4,5},{5,6},{6,7},{7,8},{8,9},{9,10},{10,1... | collective-permute-start | bytes 12296 | tf_op jit(solution)/shard_map/ppermute | solution.py:20
  11.0 5.2 %collective-permute-start.1 = (bf16[2,1024]{1,0:T(2,128)(2,1)S(1)}, bf16[2,1024]{1,0:T(2,128)(2,1)S(1)}, u32[]{:S(2)}, u32[]{:S(2)}) collective-permute-start(bf16[2,1024]{1,0:T(2,128)(2,1)S(1)} %get-tuple-element.14), channel_id=1, source_target_pairs={{1,0},{2,1},{3,2},{4,3},{5,4},{6,5},{7,6},{8,7},{9,8},{10,9},{11,1... | collective-permute-start | bytes 12296 | tf_op jit(solution)/shard_map/ppermute | solution.py:21
  17.1 85.8 %all-gather.5.cloned.1.call-start = ((), (), s32[]{:S(2)}) async-start(), calls=%async_computation.3 | async-start | bytes 1179648 | tf_op jit(solution)/shard_map/all_gather | solution.py:78
  64.5 118.6 %reduce-scatter.3.cloned.1.call-start = ((), (), s32[]{:S(2)}) async-start(), calls=%async_computation.4 | async-start | bytes 1179648 | tf_op jit(solution)/shard_map/reduce_scatter | solution.py:96
  103.0 5.0 %copy-start.2 = (bf16[128,4096]{1,0:T(8,128)(2,1)S(1)}, bf16[128,4096]{1,0:T(8,128)(2,1)}, u32[]{:S(2)}) copy-start(bf16[128,4096]{1,0:T(8,128)(2,1)} %all-gather.5.cloned.1.call-done) | copy-start | bytes 3145732
  107.9 6.6 %collective-permute-start.2 = (bf16[128,512]{1,0:T(8,128)(2,1)S(1)}, bf16[128,512]{1,0:T(8,128)(2,1)S(1)}, u32[]{:S(2)}, u32[]{:S(2)}) collective-permute-start(bf16[128,512]{1,0:T(8,128)(2,1)S(1)} %fusion.15), channel_id=1, source_target_pairs={{0,1},{1,0},{2,3},{3,2},{4,5},{5,4},{6,7},{7,6},{8,9},{9,8},{10,11... | collective-permute-start | bytes 393224 | tf_op jit(solution)/shard_map/ppermute | solution.py:29
  110.9 3.7 %collective-permute-start.3 = (bf16[128,512]{1,0:T(8,128)(2,1)S(1)}, bf16[128,512]{1,0:T(8,128)(2,1)S(1)}, u32[]{:S(2)}, u32[]{:S(2)}) collective-permute-start(bf16[128,512]{1,0:T(8,128)(2,1)S(1)} %fusion.21), channel_id=1, source_target_pairs={{0,1},{1,0},{2,3},{3,2},{4,5},{5,4},{6,7},{7,6},{8,9},{9,8},{10,11... | collective-permute-start | bytes 393224 | tf_op jit(solution)/shard_map/ppermute | solution.py:29
  115.3 67.9 %copy-start.1 = (bf16[128,512]{1,0:T(8,128)(2,1)S(1)}, bf16[128,512]{1,0:T(8,128)(2,1)}, u32[]{:S(2)}) copy-start(bf16[128,512]{1,0:T(8,128)(2,1)} %convolution_convert_fusion.2) | copy-start | bytes 393220
  120.3 135.3 %copy-start = (bf16[64,1024]{1,0:T(8,128)(2,1)S(1)}, bf16[64,1024]{1,0:T(8,128)(2,1)}, u32[]{:S(2)}) copy-start(bf16[64,1024]{1,0:T(8,128)(2,1)} %param.8) | copy-start | bytes 393220
  120.3 134.2 %reduce-scatter.5.cloned.1.call-start = ((), (), s32[]{:S(2)}) async-start(), calls=%async_computation.5 | async-start | bytes 2359296 | tf_op jit(solution)/shard_map/reduce_scatter | solution.py:100
Sparse Core Ops, SparseCore 0:
  17.3 43.2 all-gather.2
  64.6 38.2 all-gather.4
  120.4 62.7 reduce-scatter.2
  187.6 66.8 reduce-scatter.4
where the time goes:
time: 263 us
  waiting for transfers between devices  215 us (82%)
  matrix products  23 us (9%)
  between operations  13.3 us (5%)
  other arithmetic  5.48 us (2%)
  starting transfers between devices  4.4 us (2%)
    reduce_scatter x1, waiting for transfers between devices, per_device(): lax.psum_scatter(jnp.dot(mixed, w_up, preferred_element_type=jnp.float32)...  67 us
    reduce_scatter x1, waiting for transfers between devices, per_device(): lax.psum_scatter(partial_out.astype(jnp.bfloat16), 'seq', scatter_dimensi...  62.8 us
    all_gather x1, waiting for transfers between devices, per_device(): lax.all_gather(patches, 'seq', axis=0, tiled=True)  43.4 us
    all_gather x1, waiting for transfers between devices, per_device(): lax.all_gather(coarse, 'seq', axis=1, tiled=True).astype(jnp.float32)  38.4 us
  transfers between devices with their start and end apart: 8, of which 5 were waited for; matrix products, arithmetic and copies ran while one was open for 3% of the time, Pallas kernels for 0%

commit v1 on v0

--- a/solution.py
+++ b/solution.py
@@ -8,6 +8,19 @@
 HD = 128
 KW = 5
 epsilon = 1e-06
+
+
+def collect(x, axis, dim):
+    ways = lax.axis_size(axis)
+    up = [(d, (d + 1) % ways) for d in range(ways)]
+    down = [(d, (d - 1) % ways) for d in range(ways)]
+    earlier, later = ([x], [x])
+    for _ in range(ways // 2):
+        earlier.append(lax.ppermute(earlier[-1], axis, up))
+    for _ in range((ways - 1) // 2):
+        later.append(lax.ppermute(later[-1], axis, down))
+    line = jnp.concatenate([*earlier[::-1], *later[1:]], axis=dim)
+    return jnp.roll(line, (lax.axis_index(axis) - ways // 2) * x.shape[dim], axis=dim)
 
 
 def padded_2(array, sides, width):
@@ -69,11 +82,9 @@
             jnp.float32
         ) * dw_kernel[offset].astype(jnp.float32)
     patches = convolved.astype(jnp.bfloat16).reshape(frame_rows // 4, 4 * DF)
-    coarse = jnp.dot(
-        lax.all_gather(patches, "seq", axis=0, tiled=True),
-        w_down,
-        preferred_element_type=jnp.float32,
-    ).astype(jnp.bfloat16)
+    coarse = jnp.dot(collect(patches, "seq", 0), w_down, preferred_element_type=jnp.float32).astype(
+        jnp.bfloat16
+    )
     coarse_f32 = coarse.astype(jnp.float32)
     whole = lax.all_gather(coarse, "seq", axis=1, tiled=True).astype(jnp.float32)
     normed_coarse = (

time: 263 us -> 255 us (0.970)
  waiting for transfers between devices: 215 us -> 191 us
  starting transfers between devices: 4.4 us -> 20.9 us
    all_gather x1 -> x0, waiting for transfers between devices: 43.4 us -> none  [per_device(): lax.all_gather(patches, 'seq', axis=0, tiled=True)]
    ppermute x0 -> x7, waiting for transfers between devices: none -> 17.2 us  [the longest x4 16.9 us: collect(): earlier.append(lax.ppermute(earlier[-1], axis, up))]
    ppermute x0 -> x7, starting transfers between devices: none -> 16.5 us  [the longest x3 13.3 us: collect(): later.append(lax.ppermute(later[-1], axis, down))]
  transfers between devices with their start and end apart: 8 -> 14, of which waited for: 5 -> 9; matrix products, arithmetic and copies ran while one was open for 3% -> 3% of each run, Pallas kernels for 0% -> 0%
where the time goes in v1:
time: 255 us
  waiting for transfers between devices  191 us (75%)
  matrix products  22.9 us (9%)
  starting transfers between devices  20.9 us (8%)
  between operations  13.4 us (5%)
  other arithmetic  5.38 us (2%)
    reduce_scatter x1, waiting for transfers between devices, per_device(): lax.psum_scatter(jnp.dot(mixed, w_up, preferred_element_type=jnp.float32)...  66.9 us
    reduce_scatter x1, waiting for transfers between devices, per_device(): lax.psum_scatter(partial_out.astype(jnp.bfloat16), 'seq', scatter_dimensi...  63 us
    all_gather x1, waiting for transfers between devices, per_device(): lax.all_gather(coarse, 'seq', axis=1, tiled=True).astype(jnp.float32)  40.5 us
    ppermute x4, waiting for transfers between devices, collect(): earlier.append(lax.ppermute(earlier[-1], axis, up))  16.9 us
    ppermute x3, starting transfers between devices, collect(): later.append(lax.ppermute(later[-1], axis, down))  13.3 us
  transfers between devices with their start and end apart: 14, of which 9 were waited for; matrix products, arithmetic and copies ran while one was open for 3% of the time, Pallas kernels for 0%

profile of v1, /device:TPU:0, one launch (start us, length us, event | category | flops | bytes accessed | tf_op | source)
XLA Modules:
  0.0 254.6 jit_solution(14526256825828652674)
XLA Ops:
  6.5 1.0 fusion.28
  7.6 1.0 fusion.30
  8.6 2.4 collective-permute-start
  11.0 1.3 collective-permute-start.1
  12.3 0.9 slice_convert_fusion.4
  13.2 0.0 collective-permute-done
  13.2 3.0 %collective-permute-done.1 = bf16[2,1024]{1,0:T(2,128)(2,1)S(1)} collective-permute-done((bf16[2,1024]{1,0:T(2,128)(2,1)S(1)}, bf16[2,1024]{1,0:T(2,128)(2,1)S(1)}, u32[]{:S(2)}, u32[]{:S(2)}) %collective-permute-start.1) | collective-permute-done | bytes 4128 | tf_op jit(solution)/shard_map/ppermute | solution.py:34
  16.2 0.2 add_convert_fusion.1
  16.4 0.1 reshape.38
  16.5 2.3 collective-permute-start.2
  18.8 6.6 %collective-permute-done.2 = bf16[16,4096]{1,0:T(8,128)(2,1)S(1)} collective-permute-done((bf16[16,4096]{1,0:T(8,128)(2,1)S(1)}, bf16[16,4096]{1,0:T(8,128)(2,1)S(1)}, u32[]{:S(2)}, u32[]{:S(2)}) %collective-permute-start.2) | collective-permute-done | bytes 131104 | tf_op jit(solution)/shard_map/ppermute | solution.py:19
  25.4 0.0 collective-permute-start.3
  25.4 4.7 %collective-permute-start.6 = (bf16[16,4096]{1,0:T(8,128)(2,1)S(1)}, bf16[16,4096]{1,0:T(8,128)(2,1)S(1)}, u32[]{:S(2)}, u32[]{:S(2)}) collective-permute-start(bf16[16,4096]{1,0:T(8,128)(2,1)S(1)} %reshape.38), channel_id=1, source_target_pairs={{0,14},{2,0},{4,2},{6,4},{8,6},{10,8},{12,10},{14,12},{1,15},{3,1}... | collective-permute-start | bytes 393224 | tf_op jit(solution)/shard_map/ppermute | solution.py:21
  30.2 4.1 %collective-permute-done.3 = bf16[16,4096]{1,0:T(8,128)(2,1)S(1)} collective-permute-done((bf16[16,4096]{1,0:T(8,128)(2,1)S(1)}, bf16[16,4096]{1,0:T(8,128)(2,1)S(1)}, u32[]{:S(2)}, u32[]{:S(2)}) %collective-permute-start.3) | collective-permute-done | bytes 131104 | tf_op jit(solution)/shard_map/ppermute | solution.py:19
  34.2 0.3 collective-permute-start.4
  34.5 0.0 collective-permute-done.6
  34.5 4.4 %collective-permute-start.7 = (bf16[16,4096]{1,0:T(8,128)(2,1)S(1)}, bf16[16,4096]{1,0:T(8,128)(2,1)S(1)}, u32[]{:S(2)}, u32[]{:S(2)}) collective-permute-start(bf16[16,4096]{1,0:T(8,128)(2,1)S(1)} %collective-permute-done.6), channel_id=1, source_target_pairs={{0,14},{2,0},{4,2},{6,4},{8,6},{10,8},{12,10},{14,12},{1,15},{3,1}... | collective-permute-start | bytes 393224 | tf_op jit(solution)/shard_map/ppermute | solution.py:21
  38.9 3.2 %collective-permute-done.4 = bf16[16,4096]{1,0:T(8,128)(2,1)S(1)} collective-permute-done((bf16[16,4096]{1,0:T(8,128)(2,1)S(1)}, bf16[16,4096]{1,0:T(8,128)(2,1)S(1)}, u32[]{:S(2)}, u32[]{:S(2)}) %collective-permute-start.4) | collective-permute-done | bytes 131104 | tf_op jit(solution)/shard_map/ppermute | solution.py:19
  42.1 0.6 collective-permute-start.5
  42.7 4.1 %collective-permute-start.8 = (bf16[16,4096]{1,0:T(8,128)(2,1)S(1)}, bf16[16,4096]{1,0:T(8,128)(2,1)S(1)}, u32[]{:S(2)}, u32[]{:S(2)}) collective-permute-start(bf16[16,4096]{1,0:T(8,128)(2,1)S(1)} %collective-permute-done.7), channel_id=1, source_target_pairs={{0,14},{2,0},{4,2},{6,4},{8,6},{10,8},{12,10},{14,12},{1,15},{3,1}... | collective-permute-start | bytes 393224 | tf_op jit(solution)/shard_map/ppermute | solution.py:21
  46.8 3.0 %collective-permute-done.5 = bf16[16,4096]{1,0:T(8,128)(2,1)S(1)} collective-permute-done((bf16[16,4096]{1,0:T(8,128)(2,1)S(1)}, bf16[16,4096]{1,0:T(8,128)(2,1)S(1)}, u32[]{:S(2)}, u32[]{:S(2)}) %collective-permute-start.5) | collective-permute-done | bytes 131104 | tf_op jit(solution)/shard_map/ppermute | solution.py:19
  50.0 0.3 collective-permute-done.8
  50.5 0.0 copy-start.3
  50.5 3.7 %convolution_convert_fusion.2 = bf16[128,512]{1,0:T(8,128)(2,1)} fusion(bf16[4096,512]{1,0:T(8,128)(2,1)} %param.11, bf16[256,4096]{1,0:T(8,128)(2,1)S(1)} %constant_dynamic-update-slice_fusion, s32[]{:T(128)S(6)} %select_n.14), kind=kOutput, calls=%fused_computation.23 | convolution fusion | flops 536936448 | bytes 5373956 | tf_op jit(solution)/shard_map/dot_general | solution.py:85
  54.2 0.0 all-gather.2.cloned.1.call-update
  54.2 0.0 reduce-scatter.3.cloned.1.call-start
  54.2 40.5 %all-gather.2.cloned.1.call-done = bf16[128,4096]{1,0:T(8,128)(2,1)} async-done(((bf16[128,512]{1,0:T(8,128)(2,1)}), bf16[128,4096]{1,0:T(8,128)(2,1)}) %all-gather.2.cloned.1.call-update) | async-done | bytes 1048592 | tf_op jit(solution)/shard_map/all_gather | solution.py:89
  94.8 1.5 fusion.10
  96.3 3.3 %fusion.21 = bf16[128,512]{1,0:T(8,128)(2,1)S(1)} fusion(bf16[3,4096,512]{2,1,0:T(8,128)(2,1)} %param.13, bf16[128,4096]{1,0:T(8,128)(2,1)} %all-gather.2.cloned.1.call-done, f32[4096]{0:T(1024)S(1)} %copy-done.3, f32[128]{0:T(128)S(1)} %add_rsqrt_fusion), kind=kOutput, calls=%fused_computation.21 | convolution fusion | flops 539033600 | bytes 5390848 | tf_op jit(solution)/shard_map/dot_general | solution.py:96
  99.7 0.1 collective-permute-start.10
  99.7 3.0 %fusion.15 = bf16[128,512]{1,0:T(8,128)(2,1)S(1)} fusion(bf16[3,4096,512]{2,1,0:T(8,128)(2,1)} %param.13, bf16[128,4096]{1,0:T(8,128)(2,1)S(1)} %copy-done.2, f32[4096]{0:T(1024)S(1)} %copy-done.3, f32[128]{0:T(128)S(1)} %add_rsqrt_fusion), kind=kOutput, calls=%fused_computation.19 | convolution fusion | flops 539033600 | bytes 5390848 | tf_op jit(solution)/shard_map/dot_general | solution.py:99
  102.7 0.6 collective-permute-start.9
  103.3 2.9 %fusion.24 = bf16[16,4,8,128]{3,2,1,0:T(8,128)(2,1)S(1)} fusion(bf16[3,4096,512]{2,1,0:T(8,128)(2,1)} %param.13, bf16[128,4096]{1,0:T(8,128)(2,1)S(1)} %copy-done.2, f32[4096]{0:T(1024)S(1)} %copy-done.3, f32[128]{0:T(128)S(1)} %add_rsqrt_fusion), kind=kOutput, calls=%fused_computation.24 | convolution fusion | flops 539033600 | bytes 5390848 | tf_op jit(solution)/shard_map/dot_general | solution.py:93
  106.2 0.0 collective-permute-done.9
  106.3 0.1 copy.12
  106.4 0.2 convolution_multiply_fusion
  106.6 0.4 fusion.51
  107.1 1.1 convolution_convert_fusion.1
  108.1 0.0 copy-start
  108.1 3.9 %convolution_convert_fusion = bf16[128,4096]{1,0:T(8,128)(2,1)} fusion(bf16[128,512]{0,1:T(8,128)(2,1)S(1)} %bitcast.56, bf16[512,4096]{1,0:T(8,128)(2,1)} %param.14), kind=kOutput, calls=%fused_computation.1 | convolution fusion | flops 537395200 | bytes 5373952 | tf_op jit(solution)/shard_map/dot_general | solution.py:106
  112.1 0.0 reduce-scatter.3.cloned.1.call-update
  112.1 0.0 reduce-scatter.5.cloned.1.call-start
  112.1 63.0 %reduce-scatter.3.cloned.1.call-done = bf16[128,512]{1,0:T(8,128)(2,1)} async-done(((bf16[128,4096]{1,0:T(8,128)(2,1)}), bf16[128,512]{1,0:T(8,128)(2,1)}) %reduce-scatter.3.cloned.1.call-update) | async-done | bytes 131088 | tf_op jit(solution)/shard_map/reduce_scatter | solution.py:107
  175.1 4.3 %fusion.37 = f32[128,4096]{1,0:T(8,128)} fusion(bf16[512,4096]{1,0:T(8,128)(2,1)} %param.15, bf16[128,512]{1,0:T(8,128)(2,1)} %reduce-scatter.3.cloned.1.call-done, bf16[128,512]{1,0:T(8,128)(2,1)S(1)} %copy-done), kind=kOutput, calls=%fused_computation.47 | convolution fusion | flops 537133056 | bytes 6553600 | tf_op jit(solution)/shard_map/dot_general | solution.py:112
  179.5 0.0 reduce-scatter.5.cloned.1.call-update
  179.5 66.9 %reduce-scatter.5.cloned.1.call-done = f32[16,4096]{1,0:T(8,128)} async-done(((f32[128,4096]{1,0:T(8,128)}), f32[16,4096]{1,0:T(8,128)}) %reduce-scatter.5.cloned.1.call-update) | async-done | bytes 262160 | tf_op jit(solution)/shard_map/reduce_scatter | solution.py:111
  246.4 1.0 reshape.42
  247.4 0.7 fusion.31
  (29 shorter events, 0.2 us)
Async XLA Ops:
  6.5 88.2 %all-gather.2.cloned.1.call-start = ((), (), s32[]{:S(2)}) async-start(), calls=%async_computation.2 | async-start | bytes 1179648 | tf_op jit(solution)/shard_map/all_gather | solution.py:89
  8.6 4.6 %collective-permute-start = (bf16[2,1024]{1,0:T(2,128)(2,1)S(1)}, bf16[2,1024]{1,0:T(2,128)(2,1)S(1)}, u32[]{:S(2)}, u32[]{:S(2)}) collective-permute-start(bf16[2,1024]{1,0:T(2,128)(2,1)S(1)} %get-tuple-element.13), channel_id=1, source_target_pairs={{0,1},{1,2},{2,3},{3,4},{4,5},{5,6},{6,7},{7,8},{8,9},{9,10},{10,1... | collective-permute-start | bytes 12296 | tf_op jit(solution)/shard_map/ppermute | solution.py:33
  11.0 5.2 %collective-permute-start.1 = (bf16[2,1024]{1,0:T(2,128)(2,1)S(1)}, bf16[2,1024]{1,0:T(2,128)(2,1)S(1)}, u32[]{:S(2)}, u32[]{:S(2)}) collective-permute-start(bf16[2,1024]{1,0:T(2,128)(2,1)S(1)} %get-tuple-element.14), channel_id=1, source_target_pairs={{1,0},{2,1},{3,2},{4,3},{5,4},{6,5},{7,6},{8,7},{9,8},{10,9},{11,1... | collective-permute-start | bytes 12296 | tf_op jit(solution)/shard_map/ppermute | solution.py:34
  16.5 9.0 %collective-permute-start.2 = (bf16[16,4096]{1,0:T(8,128)(2,1)S(1)}, bf16[16,4096]{1,0:T(8,128)(2,1)S(1)}, u32[]{:S(2)}, u32[]{:S(2)}) collective-permute-start(bf16[16,4096]{1,0:T(8,128)(2,1)S(1)} %reshape.38), channel_id=1, source_target_pairs={{0,2},{2,4},{4,6},{6,8},{8,10},{10,12},{12,14},{14,0},{1,3},{3,5},... | collective-permute-start | bytes 393224 | tf_op jit(solution)/shard_map/ppermute | solution.py:19
  25.4 8.8 %collective-permute-start.3 = (bf16[16,4096]{1,0:T(8,128)(2,1)S(1)}, bf16[16,4096]{1,0:T(8,128)(2,1)S(1)}, u32[]{:S(2)}, u32[]{:S(2)}) collective-permute-start(bf16[16,4096]{1,0:T(8,128)(2,1)S(1)} %collective-permute-done.2), channel_id=1, source_target_pairs={{0,2},{2,4},{4,6},{6,8},{8,10},{10,12},{12,14},{14,0},{1,3},{3,5},... | collective-permute-start | bytes 393224 | tf_op jit(solution)/shard_map/ppermute | solution.py:19
  25.4 9.1 %collective-permute-start.6 = (bf16[16,4096]{1,0:T(8,128)(2,1)S(1)}, bf16[16,4096]{1,0:T(8,128)(2,1)S(1)}, u32[]{:S(2)}, u32[]{:S(2)}) collective-permute-start(bf16[16,4096]{1,0:T(8,128)(2,1)S(1)} %reshape.38), channel_id=1, source_target_pairs={{0,14},{2,0},{4,2},{6,4},{8,6},{10,8},{12,10},{14,12},{1,15},{3,1}... | collective-permute-start | bytes 393224 | tf_op jit(solution)/shard_map/ppermute | solution.py:21
  34.2 7.9 %collective-permute-start.4 = (bf16[16,4096]{1,0:T(8,128)(2,1)S(1)}, bf16[16,4096]{1,0:T(8,128)(2,1)S(1)}, u32[]{:S(2)}, u32[]{:S(2)}) collective-permute-start(bf16[16,4096]{1,0:T(8,128)(2,1)S(1)} %collective-permute-done.3), channel_id=1, source_target_pairs={{0,2},{2,4},{4,6},{6,8},{8,10},{10,12},{12,14},{14,0},{1,3},{3,5},... | collective-permute-start | bytes 393224 | tf_op jit(solution)/shard_map/ppermute | solution.py:19
  34.5 8.2 %collective-permute-start.7 = (bf16[16,4096]{1,0:T(8,128)(2,1)S(1)}, bf16[16,4096]{1,0:T(8,128)(2,1)S(1)}, u32[]{:S(2)}, u32[]{:S(2)}) collective-permute-start(bf16[16,4096]{1,0:T(8,128)(2,1)S(1)} %collective-permute-done.6), channel_id=1, source_target_pairs={{0,14},{2,0},{4,2},{6,4},{8,6},{10,8},{12,10},{14,12},{1,15},{3,1}... | collective-permute-start | bytes 393224 | tf_op jit(solution)/shard_map/ppermute | solution.py:21
  42.1 7.8 %collective-permute-start.5 = (bf16[16,4096]{1,0:T(8,128)(2,1)S(1)}, bf16[16,4096]{1,0:T(8,128)(2,1)S(1)}, u32[]{:S(2)}, u32[]{:S(2)}) collective-permute-start(bf16[16,4096]{1,0:T(8,128)(2,1)S(1)} %collective-permute-done.4), channel_id=1, source_target_pairs={{0,2},{2,4},{4,6},{6,8},{8,10},{10,12},{12,14},{14,0},{1,3},{3,5},... | collective-permute-start | bytes 393224 | tf_op jit(solution)/shard_map/ppermute | solution.py:19
  42.7 7.6 %collective-permute-start.8 = (bf16[16,4096]{1,0:T(8,128)(2,1)S(1)}, bf16[16,4096]{1,0:T(8,128)(2,1)S(1)}, u32[]{:S(2)}, u32[]{:S(2)}) collective-permute-start(bf16[16,4096]{1,0:T(8,128)(2,1)S(1)} %collective-permute-done.7), channel_id=1, source_target_pairs={{0,14},{2,0},{4,2},{6,4},{8,6},{10,8},{12,10},{14,12},{1,15},{3,1}... | collective-permute-start | bytes 393224 | tf_op jit(solution)/shard_map/ppermute | solution.py:21
  50.5 45.8 %copy-start.3 = (f32[4096]{0:T(1024)S(1)}, f32[4096]{0:T(1024)}, u32[]{:S(2)}) copy-start(f32[4096]{0:T(1024)} %param.12) | copy-start | bytes 49156
  54.2 120.9 %reduce-scatter.3.cloned.1.call-start = ((), (), s32[]{:S(2)}) async-start(), calls=%async_computation.3 | async-start | bytes 1179648 | tf_op jit(solution)/shard_map/reduce_scatter | solution.py:107
  96.3 3.4 %copy-start.2 = (bf16[128,4096]{1,0:T(8,128)(2,1)S(1)}, bf16[128,4096]{1,0:T(8,128)(2,1)}, u32[]{:S(2)}) copy-start(bf16[128,4096]{1,0:T(8,128)(2,1)} %all-gather.2.cloned.1.call-done) | copy-start | bytes 3145732
  99.7 6.7 %collective-permute-start.10 = (bf16[128,512]{1,0:T(8,128)(2,1)S(1)}, bf16[128,512]{1,0:T(8,128)(2,1)S(1)}, u32[]{:S(2)}, u32[]{:S(2)}) collective-permute-start(bf16[128,512]{1,0:T(8,128)(2,1)S(1)} %fusion.21), channel_id=1, source_target_pairs={{0,1},{1,0},{2,3},{3,2},{4,5},{5,4},{6,7},{7,6},{8,9},{9,8},{10,11... | collective-permute-start | bytes 393224 | tf_op jit(solution)/shard_map/ppermute | solution.py:42
  102.7 3.5 %collective-permute-start.9 = (bf16[128,512]{1,0:T(8,128)(2,1)S(1)}, bf16[128,512]{1,0:T(8,128)(2,1)S(1)}, u32[]{:S(2)}, u32[]{:S(2)}) collective-permute-start(bf16[128,512]{1,0:T(8,128)(2,1)S(1)} %fusion.15), channel_id=1, source_target_pairs={{0,1},{1,0},{2,3},{3,2},{4,5},{5,4},{6,7},{7,6},{8,9},{9,8},{10,11... | collective-permute-start | bytes 393224 | tf_op jit(solution)/shard_map/ppermute | solution.py:42
  108.1 67.0 %copy-start = (bf16[128,512]{1,0:T(8,128)(2,1)S(1)}, bf16[128,512]{1,0:T(8,128)(2,1)}, u32[]{:S(2)}) copy-start(bf16[128,512]{1,0:T(8,128)(2,1)} %convolution_convert_fusion.2) | copy-start | bytes 393220
  112.1 134.3 %reduce-scatter.5.cloned.1.call-start = ((), (), s32[]{:S(2)}) async-start(), calls=%async_computation.4 | async-start | bytes 2359296 | tf_op jit(solution)/shard_map/reduce_scatter | solution.py:111
  179.4 68.0 %copy-start.1 = (bf16[64,1024]{1,0:T(8,128)(2,1)S(1)}, bf16[64,1024]{1,0:T(8,128)(2,1)}, u32[]{:S(2)}) copy-start(bf16[64,1024]{1,0:T(8,128)(2,1)} %param.8) | copy-start | bytes 393220
Sparse Core Ops, SparseCore 0:
  54.3 40.4 all-gather.1
  112.2 62.8 reduce-scatter.2
  179.6 66.7 reduce-scatter.4
